TPU v7x, 128 devices: a whole 4x4x4 slice. The times are simulated.
128 devices in a mesh: slab: 8 (over x, y_hi), plane: 16 (over z, y_lo, core).
Axes of the slice: x: 4, y: 4 (y_hi: 2, y_lo: 2; y = y_hi * 2 + y_lo), z: 4, core: 2. Of those that a mesh axis runs over, the one named last changes fastest.
Arguments:
- images: float32 [2, 64, 256, 1024], P(None, 'slab', 'plane'), may hold values from -12 to 12, as said below
- shifts: int32 [3, 8, 32, 128], P(None, 'slab', 'plane'), may hold values from -1 to 1
- initial_displacement: float32 [3, 8, 32, 128], P(None, 'slab', 'plane'), may hold values from -2 to 2
Outputs:
- displacement: float32 [3, 8, 32, 128], P(None, 'slab', 'plane')
- mismatch: float32 [64, 256, 1024], P('slab', 'plane')
Inputs may be any that keep to these rules, and one draw needn't show every extreme that they name: `images`: voxel intensities.
All inputs are finite; a program needn't handle non-finite values.
Results may differ from a plain program's by a relative error of at most 0.0023.
Values sent between devices are 32-bit elements; how exact they have to be, the bound alone decides.
No kernel may reach another device: no remote copies, remote signals or barrier semaphores. Data moves between devices by JAX's collectives and lax.ppermute only.
A program may use at most 192 MiB of HBM per device.

v0:
```python
import jax
import jax.numpy as jnp
from jax import lax
from jax.sharding import PartitionSpec as P

ELEM = 8
ITERS = 6


reg_weight = 4.0


def shifted(value, axis, steps):
    count = lax.axis_size(axis)
    initial, last = (max(0, -steps), min(count, count - steps))
    return lax.ppermute(value, axis, [(source, source + steps) for source in range(initial, last)])


def extended(block, sides, width):
    for axis, dim in sides:
        count = lax.axis_size(axis)
        forward = [(i, i + 1) for i in range(count - 1)]
        backward = [(target, source) for source, target in forward]
        low = lax.ppermute(
            lax.slice_in_dim(block, block.shape[dim] - width, None, axis=dim), axis, forward
        )
        high = lax.ppermute(lax.slice_in_dim(block, 0, width, axis=dim), axis, backward)
        block = jnp.concatenate([low, block, high], axis=dim)
    return block


def edge_weights():
    return jnp.arange(ELEM, dtype=jnp.float32) / ELEM


def interpolate(padded):
    weights = edge_weights()
    lower_w = 1.0 - weights
    comps, nodes_z, nodes_y, nodes_x = padded.shape
    depth_direction = (
        padded[:, :-1, None] * lower_w[:, None, None] + padded[:, 1:, None] * weights[:, None, None]
    )
    depth_direction = depth_direction.reshape(comps, (nodes_z - 1) * ELEM, nodes_y, nodes_x)
    along_y = (
        depth_direction[:, :, :-1, None] * lower_w[:, None]
        + depth_direction[:, :, 1:, None] * weights[:, None]
    )
    along_y = along_y.reshape(comps, (nodes_z - 1) * ELEM, (nodes_y - 1) * ELEM, nodes_x)
    along_x = along_y[..., :-1, None] * lower_w + along_y[..., 1:, None] * weights
    return along_x.reshape(comps, (nodes_z - 1) * ELEM, (nodes_y - 1) * ELEM, (nodes_x - 1) * ELEM)


def laplacian(padded):
    centre = padded[:, 1:-1, 1:-1, 1:-1]
    beside = padded[:, :-2, 1:-1, 1:-1] + padded[:, 2:, 1:-1, 1:-1]
    beside = beside + padded[:, 1:-1, :-2, 1:-1] + padded[:, 1:-1, 2:, 1:-1]
    beside = beside + padded[:, 1:-1, 1:-1, :-2] + padded[:, 1:-1, 1:-1, 2:]
    return 6.0 * centre - beside


def collapse_width(field):
    weights = edge_weights()
    comps, zcount, ycount, xcount = field.shape
    blocks = field.reshape(comps, zcount, ycount, xcount // ELEM, ELEM)
    lower = jnp.sum(blocks * (1.0 - weights), -1)
    upper = jnp.sum(blocks * weights, -1)
    return lower + jnp.concatenate([jnp.zeros_like(upper[..., :1]), upper[..., :-1]], -1)


def reduce_y(field):
    weights = edge_weights()
    comps, zcount, ycount, xcount = field.shape
    blocks = field.reshape(comps, zcount, ycount // ELEM, ELEM, xcount)
    lower = jnp.sum(blocks * (1.0 - weights)[:, None], 3)
    upper = jnp.sum(blocks * weights[:, None], 3)
    return (lower, upper)


def reduce_z(field):
    weights = edge_weights()
    comps, zcount, ycount, xcount = field.shape
    blocks = field.reshape(comps, zcount // ELEM, ELEM, ycount, xcount)
    lower = jnp.sum(blocks * (1.0 - weights)[:, None, None], 2)
    upper = jnp.sum(blocks * weights[:, None, None], 2)
    return (lower, upper)


def assemble(field):
    nodes_x = collapse_width(field)
    lower, upper = reduce_y(nodes_x)
    carried = shifted(upper[:, :, -1:], "plane", 1)
    nodes_y = lower + jnp.concatenate([carried, upper[:, :, :-1]], 2)
    lower, upper = reduce_z(nodes_y)
    carried = shifted(upper, "slab", 1)
    return lower + jnp.concatenate([carried, upper[:, :-1]], 1)


def gradient(padded, margin, zcount, ycount, xcount):

    def piece(off_z, off_y, off_x):
        return padded[
            margin + off_z : margin + off_z + zcount,
            margin + off_y : margin + off_y + ycount,
            margin + off_x : margin + off_x + xcount,
        ]

    grad_z = (
        piece(-2, 0, 0) - 8.0 * piece(-1, 0, 0) + 8.0 * piece(1, 0, 0) - piece(2, 0, 0)
    ) / 12.0
    gradient_height = (
        piece(0, -2, 0) - 8.0 * piece(0, -1, 0) + 8.0 * piece(0, 1, 0) - piece(0, 2, 0)
    ) / 12.0
    grad_x = (
        piece(0, 0, -2) - 8.0 * piece(0, 0, -1) + 8.0 * piece(0, 0, 1) - piece(0, 0, 2)
    ) / 12.0
    return jnp.stack([grad_z, gradient_height, grad_x])


def voxel_codes(shifts):
    codes = (shifts[0] + 1) * 9 + (shifts[1] + 1) * 3 + (shifts[2] + 1)
    elem_z, elem_y, elem_x = codes.shape
    spread = jnp.broadcast_to(
        codes[:, None, :, None, :, None], (elem_z, ELEM, elem_y, ELEM, elem_x, ELEM)
    )
    return spread.reshape(elem_z * ELEM, elem_y * ELEM, elem_x * ELEM)


def warp_image(padded, margin, codes):
    zcount, ycount, xcount = codes.shape
    result = jnp.zeros(codes.shape, padded.dtype)
    for candidate in range(27):
        off_z = candidate // 9 - 1
        off_y = candidate // 3 % 3 - 1
        off_x = candidate % 3 - 1
        piece = padded[
            margin + off_z : margin + off_z + zcount,
            margin + off_y : margin + off_y + ycount,
            margin + off_x : margin + off_x + xcount,
        ]
        result = jnp.where(codes == candidate, piece, result)
    return result


def rim_nodes(vector):
    return extended(vector, (("slab", 1), ("plane", 2)), 1)


def node_parts(vector):
    rimmed = rim_nodes(vector)
    upper_side = jnp.pad(rimmed[:, 1:, 1:, :], ((0, 0), (0, 0), (0, 0), (0, 1)))
    both_sides = jnp.pad(rimmed, ((0, 0), (0, 0), (0, 0), (1, 1)))
    return (interpolate(upper_side), laplacian(both_sides))


def residual_norm(residual, counted):
    return lax.psum(jnp.sum(residual * residual * counted), ("slab", "plane"))


def body(images, shifts, initial_displacement):
    plane_count = images.shape[1]
    row_count = images.shape[2]
    column_count = images.shape[3]
    codes = voxel_codes(shifts)
    rimmed = extended(images, (("slab", 1), ("plane", 2)), 2)
    rimmed = jnp.pad(rimmed, ((0, 0), (0, 0), (0, 0), (2, 2)))
    grads = gradient(rimmed[0], 2, plane_count, row_count, column_count)
    warped = warp_image(rimmed[1], 2, codes)
    energy = lax.psum(jnp.sum(grads * grads), ("slab", "plane"))
    voxel_total = (
        plane_count * row_count * column_count * lax.axis_size("slab") * lax.axis_size("plane")
    )
    smoothing_penalty = reg_weight * energy / voxel_total
    counted = 1.0
    moved, lap_start = node_parts(initial_displacement)
    mismatch = images[0] - warped - jnp.sum(grads * moved, 0)
    rhs = assemble(grads * mismatch[None]) - smoothing_penalty * lap_start
    step = jnp.zeros_like(rhs)
    residual = rhs
    direction = rhs
    norm_now = residual_norm(residual, counted)
    for sweep in range(ITERS):
        flow, lap_part = node_parts(direction)
        scalar = jnp.sum(grads * flow, 0)
        applied = assemble(grads * scalar[None]) + smoothing_penalty * lap_part
        step_size = norm_now / lax.psum(jnp.sum(direction * applied * counted), ("slab", "plane"))
        step = step + step_size * direction
        residual = residual - step_size * applied
        norm_next = residual_norm(residual, counted)
        direction = residual + norm_next / norm_now * direction
        norm_now = norm_next
    return (initial_displacement + step, mismatch)


def solution(mesh):
    in_specs = (
        P(None, "slab", "plane", None),
        P(None, "slab", "plane", None),
        P(None, "slab", "plane", None),
    )
    out_specs = (P(None, "slab", "plane", None), P("slab", "plane", None))
    return jax.shard_map(body, mesh=mesh, in_specs=in_specs, out_specs=out_specs, check_vma=False)
```

profile of v0, /device:TPU:1, one launch (start us, length us, event | category | flops | bytes accessed | tf_op | source)
XLA Modules:
  0.0 1258.1 jit_solution(13060840609675281188)
XLA Ops:
  2.1 6.3 collective-permute-start.4
  10.1 5.8 collective-permute-start
  27.7 3.9 collective-permute-start.6
  76.9 3.1 collective-permute-start.2
  80.8 6.7 copy.423
  87.4 6.6 copy.424
  94.1 6.5 copy.422
  100.6 19.2 %select_maximum_fusion = f32[2,12,20,1028]{2,3,1,0:T(8,128)} fusion(f32[2,12,2,1024]{2,3,1,0:T(8,128)} %copy.424, f32[2,12,16,1024]{2,3,1,0:T(8,128)} %copy.423, f32[2,12,2,1024]{2,3,1,0:T(8,128)} %copy.422), kind=kLoop, calls=%fused_computation.2 | loop fusion | flops 3947520 | bytes 3939840 | tf_op jit(solution)/shard_map/concatenate | solution.py:28
  119.7 8.1 slice_bitcast_fusion.1
  127.8 14.7 %fusion.34 = (f32[8,16,1024]{1,2,0:T(8,128)}, f32[8,16,1024]{1,2,0:T(8,128)}, f32[8,16,1024]{1,2,0:T(8,128)}) fusion(f32[12,20,1028]{1,2,0:T(8,128)S(1)} %get-tuple-element.81), kind=kLoop, calls=%fused_computation.49 | loop fusion | flops 2359296 | bytes 7864320 | tf_op jit(solution)/shard_map/div | solution.py:107
  154.4 59.1 %fusion.27 = f32[8,16,1024]{1,2,0:T(8,128)} fusion(f32[12,20,1028]{1,2,0:T(8,128)} %get-tuple-element.82, f32[8,16,128,8]{1,3,2,0:T(8,128)} %copy.459, f32[1,8,16,1024]{2,3,1,0:T(8,128)} %copy.524, pred[16,1024]{0,1:T(8,128)(4,1)S(1)} %copy.455, pred[16,1024]{0,1:T(8,128)(4,1)S(1)} %copy-done.2, pred[16,1024]{0,1:T(8,128)(4,1)S(1)} %copy-done.3, ...), kind=kLoop, calls=%fused_computation.35 | loop fusion | flops 3801088 | bytes 16171008 | tf_op jit(solution)/shard_map/sub | solution.py:175
  237.3 5.9 collective-permute-start.8
  244.1 65.6 %psum.91 = f32[]{:T(128)} all-reduce(f32[]{:T(128)} %fusion.37), channel_id=1, replica_groups=mesh['slab'=8,'plane'=16] {'slab','plane'}, use_global_device_ids=true, to_apply=%region_8.9 | all-reduce | flops 1 | bytes 8 | tf_op jit(solution)/shard_map/psum | solution.py:168
  312.4 5.5 collective-permute-start.10
  319.2 3.9 collective-permute-start.12
  336.1 3.9 collective-permute-start.15
  340.1 5.4 collective-permute-start.14
  346.9 66.6 %all-reduce.22 = (f32[]{:T(128)}, f32[]{:T(128)}) all-reduce(f32[]{:T(128)} %get-tuple-element.61, f32[]{:T(128)} %get-tuple-element.60), channel_id=1, replica_groups=mesh['slab'=8,'plane'=16] {'slab','plane'}, use_global_device_ids=true, to_apply=%region_10.11 | all-reduce | flops 2 | bytes 16 | tf_op jit(solution)/shard_map/psum | solution.py:156
  415.5 63.6 %psum.94 = f32[]{:T(128)} all-reduce(f32[]{:T(128)} %multiply_reduce_fusion.43), channel_id=1, replica_groups=mesh['slab'=8,'plane'=16] {'slab','plane'}, use_global_device_ids=true, to_apply=%region_21.22 | all-reduce | flops 1 | bytes 8 | tf_op jit(solution)/shard_map/psum | solution.py:156
  481.7 5.5 collective-permute-start.16
  488.5 3.9 collective-permute-start.18
  508.5 5.6 collective-permute-start.20
  515.5 66.8 %psum.95 = f32[]{:T(128)} all-reduce(f32[]{:T(128)} %get-tuple-element.76), channel_id=1, replica_groups=mesh['slab'=8,'plane'=16] {'slab','plane'}, use_global_device_ids=true, to_apply=%region_30.31 | all-reduce | flops 1 | bytes 8 | tf_op jit(solution)/shard_map/psum | solution.py:185
  584.3 63.6 %psum.96 = f32[]{:T(128)} all-reduce(f32[]{:T(128)} %get-tuple-element.74), channel_id=1, replica_groups=mesh['slab'=8,'plane'=16] {'slab','plane'}, use_global_device_ids=true, to_apply=%region_32.33 | all-reduce | flops 1 | bytes 8 | tf_op jit(solution)/shard_map/psum | solution.py:156
  650.5 5.5 collective-permute-start.22
  657.4 3.9 collective-permute-start.24
  674.2 3.0 collective-permute-start.27
  677.4 5.4 collective-permute-start.26
  684.2 66.6 %psum.97 = f32[]{:T(128)} all-reduce(f32[]{:T(128)} %get-tuple-element.72), channel_id=1, replica_groups=mesh['slab'=8,'plane'=16] {'slab','plane'}, use_global_device_ids=true, to_apply=%region_41.42 | all-reduce | flops 1 | bytes 8 | tf_op jit(solution)/shard_map/psum | solution.py:185
  752.7 63.6 %psum.98 = f32[]{:T(128)} all-reduce(f32[]{:T(128)} %get-tuple-element.70), channel_id=1, replica_groups=mesh['slab'=8,'plane'=16] {'slab','plane'}, use_global_device_ids=true, to_apply=%region_43.44 | all-reduce | flops 1 | bytes 8 | tf_op jit(solution)/shard_map/psum | solution.py:156
  818.9 5.5 collective-permute-start.28
  825.8 3.9 collective-permute-start.30
  842.6 3.2 collective-permute-start.33
  845.9 5.4 collective-permute-start.32
  852.7 66.6 %psum.99 = f32[]{:T(128)} all-reduce(f32[]{:T(128)} %get-tuple-element.68), channel_id=1, replica_groups=mesh['slab'=8,'plane'=16] {'slab','plane'}, use_global_device_ids=true, to_apply=%region_52.53 | all-reduce | flops 1 | bytes 8 | tf_op jit(solution)/shard_map/psum | solution.py:185
  921.3 63.6 %psum.100 = f32[]{:T(128)} all-reduce(f32[]{:T(128)} %get-tuple-element.66), channel_id=1, replica_groups=mesh['slab'=8,'plane'=16] {'slab','plane'}, use_global_device_ids=true, to_apply=%region_54.55 | all-reduce | flops 1 | bytes 8 | tf_op jit(solution)/shard_map/psum | solution.py:156
  987.5 5.5 collective-permute-start.34
  994.4 3.9 collective-permute-start.36
  1011.2 3.2 collective-permute-start.39
  1014.5 5.4 collective-permute-start.38
  1021.3 66.4 %psum.101 = f32[]{:T(128)} all-reduce(f32[]{:T(128)} %get-tuple-element.64), channel_id=1, replica_groups=mesh['slab'=8,'plane'=16] {'slab','plane'}, use_global_device_ids=true, to_apply=%region_63.64 | all-reduce | flops 1 | bytes 8 | tf_op jit(solution)/shard_map/psum | solution.py:185
  1089.7 63.6 %psum.102 = f32[]{:T(128)} all-reduce(f32[]{:T(128)} %multiply_reduce_fusion.35), channel_id=1, replica_groups=mesh['slab'=8,'plane'=16] {'slab','plane'}, use_global_device_ids=true, to_apply=%region_65.66 | all-reduce | flops 1 | bytes 8 | tf_op jit(solution)/shard_map/psum | solution.py:156
  1155.9 5.5 collective-permute-start.40
  1162.1 3.9 collective-permute-start.42
  1175.8 3.2 collective-permute-start.45
  1179.1 5.4 collective-permute-start.44
  1186.0 3.5 copy.509
  1189.5 66.4 %psum.103 = f32[]{:T(128)} all-reduce(f32[]{:T(128)} %fusion.103), channel_id=1, replica_groups=mesh['slab'=8,'plane'=16] {'slab','plane'}, use_global_device_ids=true, to_apply=%region_74.75 | all-reduce | flops 1 | bytes 8 | tf_op jit(solution)/shard_map/psum | solution.py:185
  (482 shorter events, 201.7 us)
Async XLA Ops:
  0.6 26.4 %collective-permute-start.5 = (f32[3,1,2,128]{3,2,0,1:T(2,128)}, f32[3,1,2,128]{3,2,0,1:T(2,128)S(1)}, u32[]{:S(2)}, u32[]{:S(2)}) collective-permute-start(f32[3,1,2,128]{3,2,0,1:T(2,128)} %bitcast.337), channel_id=1, source_target_pairs={{16,0},{32,16},{48,32},{64,48},{80,64},{96,80},{112,96},{17,1},{33... | collective-permute-start | bytes 9224 | tf_op jit(solution)/shard_map/ppermute | solution.py:27
  2.1 25.0 %collective-permute-start.4 = (f32[3,1,2,128]{3,2,0,1:T(2,128)}, f32[3,1,2,128]{3,2,0,1:T(2,128)S(1)}, u32[]{:S(2)}, u32[]{:S(2)}) collective-permute-start(f32[3,1,2,128]{3,2,0,1:T(2,128)} %bitcast.338), channel_id=1, source_target_pairs={{0,16},{16,32},{32,48},{48,64},{64,80},{80,96},{96,112},{1,17},{17... | collective-permute-start | bytes 9224 | tf_op jit(solution)/shard_map/ppermute | solution.py:24
  10.1 63.7 %collective-permute-start = (f32[2,2,16,1024]{3,2,1,0:T(8,128)S(1)}, f32[2,2,16,1024]{3,2,1,0:T(8,128)S(1)}, u32[]{:S(2)}, u32[]{:S(2)}) collective-permute-start(f32[2,2,16,1024]{3,2,1,0:T(8,128)S(1)} %get-tuple-element.89), channel_id=1, source_target_pairs={{0,16},{16,32},{32,48},{48,64},{64,80},{80,96},{96,112},{1,17},{17... | collective-permute-start | bytes 786440 | tf_op jit(solution)/shard_map/ppermute | solution.py:24
  15.9 58.1 %collective-permute-start.1 = (f32[2,2,16,1024]{3,2,1,0:T(8,128)}, f32[2,2,16,1024]{3,2,1,0:T(8,128)S(1)}, u32[]{:S(2)}, u32[]{:S(2)}) collective-permute-start(f32[2,2,16,1024]{3,2,1,0:T(8,128)} %get-tuple-element.88), channel_id=1, source_target_pairs={{16,0},{32,16},{48,32},{64,48},{80,64},{96,80},{112,96},{17,1},{33... | collective-permute-start | bytes 786440 | tf_op jit(solution)/shard_map/ppermute | solution.py:27
  27.0 216.2 %copy-start.25 = (f32[3,1,2,128]{3,2,0,1:T(2,128)}, f32[3,1,2,128]{3,2,0,1:T(2,128)S(1)}, u32[]{:S(2)}) copy-start(f32[3,1,2,128]{3,2,0,1:T(2,128)S(1)} %collective-permute-done.5) | copy-start | bytes 9220
  27.7 45.2 %collective-permute-start.6 = (f32[3,3,1,128]{3,2,0,1:T(1,128)S(1)}, f32[3,3,1,128]{3,2,0,1:T(1,128)S(1)}, u32[]{:S(2)}, u32[]{:S(2)}) collective-permute-start(f32[3,3,1,128]{3,2,0,1:T(1,128)S(1)} %get-tuple-element.159), channel_id=1, source_target_pairs={{1,0},{2,1},{3,2},{4,3},{5,4},{6,5},{7,6},{8,7},{9,8},{10,9},{11,1... | collective-permute-start | bytes 13832 | tf_op jit(solution)/shard_map/ppermute | solution.py:27
  70.7 172.6 %collective-permute-start.9 = (f32[3,3,1,128]{3,2,0,1:T(1,128)}, f32[3,3,1,128]{3,2,0,1:T(1,128)}, u32[]{:S(2)}, u32[]{:S(2)}) collective-permute-start(f32[3,3,1,128]{3,2,0,1:T(1,128)} %get-tuple-element.158), channel_id=1, source_target_pairs={{0,1},{1,2},{2,3},{3,4},{4,5},{5,6},{6,7},{7,8},{8,9},{9,10},{10,1... | collective-permute-start | bytes 13832 | tf_op jit(solution)/shard_map/ppermute | solution.py:24
  74.2 13.3 %collective-permute-start.3 = (f32[2,12,2,1024]{3,2,1,0:T(2,128)S(1)}, f32[2,12,2,1024]{3,2,1,0:T(2,128)S(1)}, u32[]{:S(2)}, u32[]{:S(2)}) collective-permute-start(f32[2,12,2,1024]{3,2,1,0:T(2,128)S(1)} %get-tuple-element.87), channel_id=1, source_target_pairs={{1,0},{2,1},{3,2},{4,3},{5,4},{6,5},{7,6},{8,7},{9,8},{10,9},{11,1... | collective-permute-start | bytes 589832 | tf_op jit(solution)/shard_map/ppermute | solution.py:27
  76.9 17.2 %collective-permute-start.2 = (f32[2,12,2,1024]{3,2,1,0:T(2,128)S(1)}, f32[2,12,2,1024]{3,2,1,0:T(2,128)S(1)}, u32[]{:S(2)}, u32[]{:S(2)}) collective-permute-start(f32[2,12,2,1024]{3,2,1,0:T(2,128)S(1)} %get-tuple-element.86), channel_id=1, source_target_pairs={{0,1},{1,2},{2,3},{3,4},{4,5},{5,6},{6,7},{7,8},{8,9},{9,10},{10,1... | collective-permute-start | bytes 589832 | tf_op jit(solution)/shard_map/ppermute | solution.py:24
  224.7 12.4 collective-permute-start.7
  237.3 73.0 %collective-permute-start.8 = (f32[3,1,2,128]{3,2,0,1:T(2,128)S(1)}, f32[3,1,2,128]{3,2,0,1:T(2,128)S(1)}, u32[]{:S(2)}, u32[]{:S(2)}) collective-permute-start(f32[3,1,2,128]{3,2,0,1:T(2,128)S(1)} %bitcast.357), channel_id=1, source_target_pairs={{0,16},{16,32},{32,48},{48,64},{64,80},{80,96},{96,112},{1,17},{17... | collective-permute-start | bytes 9224 | tf_op jit(solution)/shard_map/ppermute | solution.py:16
  311.1 6.8 collective-permute-start.11
  312.4 6.2 collective-permute-start.10
  319.2 5.0 collective-permute-start.12
  332.0 162.3 %copy-start.71 = (f32[16]{0:T(128)S(1)}, f32[16]{0:T(128)}, u32[]{:S(2)}) copy-start(f32[16]{0:T(128)} %copy-done.69) | copy-start | bytes 196
  334.1 5.9 collective-permute-start.13
  336.1 9.4 collective-permute-start.15
  340.1 6.1 collective-permute-start.14
  480.4 6.8 collective-permute-start.17
  481.7 6.2 collective-permute-start.16
  488.5 4.9 collective-permute-start.18
  503.4 5.0 collective-permute-start.19
  505.4 8.7 collective-permute-start.21
  508.5 6.3 collective-permute-start.20
  649.2 6.8 collective-permute-start.23
  650.5 6.2 collective-permute-start.22
  657.4 4.9 collective-permute-start.24
  672.2 5.0 collective-permute-start.25
  674.2 8.6 collective-permute-start.27
  677.4 6.1 collective-permute-start.26
  817.6 6.8 collective-permute-start.29
  818.9 6.2 collective-permute-start.28
  825.8 4.9 collective-permute-start.30
  840.6 5.1 collective-permute-start.31
  842.6 8.7 collective-permute-start.33
  845.9 6.1 collective-permute-start.32
  986.2 6.8 collective-permute-start.35
  987.5 6.2 collective-permute-start.34
  994.4 4.9 collective-permute-start.36
  1009.2 5.1 collective-permute-start.37
  1011.2 8.7 collective-permute-start.39
  1014.5 6.1 collective-permute-start.38
  1154.6 6.8 collective-permute-start.41
  1155.9 6.2 collective-permute-start.40
  1162.1 4.9 collective-permute-start.42
  1173.8 5.1 collective-permute-start.43
  1175.8 8.7 collective-permute-start.45
  1179.1 6.1 collective-permute-start.44
  (80 other events, 3115.3 us)
where the time goes:
time: 1270 us; the launch traced here: 1260 us
  blocking collectives  783 us (62%)
  starting transfers between devices  163 us (13%)
  local copies, waits for them, and re-layouts  140 us (11%)
  other arithmetic  139 us (11%)
  between operations  18.8 us (1%)
  waiting for transfers between devices  13.6 us (1%)
    psum x6, blocking collectives, residual_norm(): return lax.psum(jnp.sum(residual * residual * counted), ('slab', 'plane'))  384 us
    psum x5, blocking collectives, body(): lax.psum(jnp.sum(direction * applied * counted), ('slab', 'plane'))  333 us
    ppermute x16, starting transfers between devices, extended(): lax.ppermute(lax.slice_in_dim(block, block.shape[dim] - width, None, axis...  69.7 us
    psum x1, blocking collectives, body(): energy = lax.psum(jnp.sum(grads * grads), ('slab', 'plane'))  65.6 us
    sub x1, other arithmetic, body(): mismatch = images[0] - warped - jnp.sum(grads * moved, 0)  59.1 us
    ppermute x14, starting transfers between devices, shifted(): lax.ppermute(value, axis, [(source, source + steps) for source in range(i...  53.2 us
    eq x54, local copies, waits for them, and re-layouts, warp_image(): result = jnp.where(codes == candidate, piece, result)  40.6 us
    ppermute x16, starting transfers between devices, extended(): lax.ppermute(lax.slice_in_dim(block, 0, width, axis=dim), axis, backward)  40.5 us
  transfers between devices with their start and end apart: 46, of which 18 were waited for; matrix products, arithmetic and copies ran while one was open for 17% of the time, Pallas kernels for 0%

commit v1 on v0

v1 whole, which is shorter than its diff:
```python
import jax
import jax.numpy as jnp
import numpy as np
from jax import lax
from jax.experimental import pallas as pl
from jax.experimental.pallas import tpu as pltpu
from jax.sharding import PartitionSpec as P

ELEM = 8
ITERS = 6
reg_weight = 4.0
AXES = ("slab", "plane")
NCHUNK = 8
ROWS = 112
RHS_ROW = 96
U_ROW = 102
ENERGY_ROW = 108
COLORS = ((0, 40), (40, 40), (80, 32))
STRIDE = 136
PAIRS = ((0, 0), (0, 1), (0, 2), (1, 1), (1, 2), (2, 2))
AB = [[0, 1, 2], [1, 3, 4], [2, 4, 5]]
F32 = jnp.float32
BF16 = jnp.bfloat16


def build_constants():
    w = np.arange(8) / 8.0
    lo, up = 1.0 - w, w
    quad = (lo * lo, lo * up, up * up)
    lin = (lo, up)
    wq = np.zeros((1024, 256))
    wl = np.zeros((1024, 128))
    for e in range(128):
        for i in range(8):
            v = 8 * e + i
            wq[v, e] += quad[0][i]
            wq[v, 128 + e] += quad[1][i]
            wl[v, e] += lin[0][i]
            if e + 1 < 128:
                wq[v, e + 1] += quad[2][i]
                wl[v, e + 1] += lin[1][i]
    spread = np.zeros((128, 1024))
    for e in range(128):
        spread[e, 8 * e : 8 * e + 8] = 1.0
    ly = np.zeros((4, 48, 288))
    ry = np.zeros((4, 8, 96))

    def put(which, tz, yk, zt, er, yq):
        for ab in range(6):
            for s in range(8):
                ly[which, (tz * 4 + yk) * 6 + ab, ((zt * 6 + ab) * 2 + er) * 8 + s] += quad[yq][s]

    for which, tz, zt in ((0, 0, 0), (0, 1, 1), (1, 0, 2)):
        put(which, tz, 0, zt, 0, 0)
        put(which, tz, 1, zt, 0, 2)
        put(which, tz, 1, zt, 1, 0)
        put(which, tz, 2, zt, 0, 1)
        put(which, tz, 3, zt, 1, 1)
    for which, tz, zt in ((2, 0, 0), (2, 1, 1), (3, 0, 2)):
        put(which, tz, 0, zt, 1, 2)

    def put_rhs(which, yl, zt, er, yq):
        for c in range(3):
            for s in range(8):
                ry[which, yl * 3 + c, ((zt * 3 + c) * 2 + er) * 8 + s] += lin[yq][s]

    for which, zt in ((0, 0), (1, 1)):
        put_rhs(which, 0, zt, 0, 0)
        put_rhs(which, 1, zt, 0, 1)
        put_rhs(which, 1, zt, 1, 0)
    for which, zt in ((2, 0), (3, 1)):
        put_rhs(which, 0, zt, 1, 1)
    cast = lambda a: jnp.asarray(a.astype(np.float32)).astype(BF16)
    return (
        cast(wq),
        cast(wl),
        cast(wl.T),
        cast(spread),
        cast(ly.reshape(192, 288)),
        cast(ry.reshape(32, 96)),
    )


def dot(a, b):
    return lax.dot_general(a, b, (((1,), (0,)), ((), ())), preferred_element_type=F32)


def split_left(a, b, parts=2):
    total = None
    for _ in range(parts):
        piece = a.astype(BF16)
        a = a - piece.astype(F32)
        term = dot(piece, b)
        total = term if total is None else total + term
    return total


def split_right(a, b, parts=2):
    total = None
    for _ in range(parts):
        piece = b.astype(BF16)
        b = b - piece.astype(F32)
        term = dot(a, piece)
        total = term if total is None else total + term
    return total


def local_kernel(
    images, zlo, zhi, ylo, yhi, shifts, nodes, wq, wl, wi, spread, ly, ry,
    mismatch, own, to_slab, to_plane, to_both,
    pad0, pad1, gx, sh, un, acc, acc_rhs,
):
    lane = lax.broadcasted_iota(jnp.int32, (1, 1024), 1)
    pad0[2:10, 8:24, :] = images[0]
    pad0[0:2, 8:24, :] = zlo[0:32, :].reshape(2, 16, 1024)
    pad0[10:12, 8:24, :] = zhi[0:32, :].reshape(2, 16, 1024)
    pad1[1, 0, 8:24, :] = zlo[32:48, :]
    pad1[1, 1:9, 8:24, :] = images[1]
    pad1[1, 9, 8:24, :] = zhi[32:48, :]
    for z in range(8):
        pad0[2 + z, 6:8, :] = ylo[2 * z : 2 * z + 2, :]
        pad0[2 + z, 24:26, :] = yhi[2 * z : 2 * z + 2, :]
    for k in range(10):
        pad1[1, k, 7:8, :] = ylo[16 + k : 17 + k, :]
        pad1[1, k, 24:25, :] = yhi[16 + k : 17 + k, :]

    def lanes(value, off):
        moved = pltpu.roll(value, (-off) % 1024, value.ndim - 1)
        inside = (lane + off >= 0) & (lane + off < 1024)
        return jnp.where(inside, moved, 0.0)

    def shift_planes(k, carry):
        plane = pad1[1, k]
        pad1[0, k] = lanes(plane, -1)
        pad1[2, k] = lanes(plane, 1)
        return carry

    lax.fori_loop(0, 10, shift_planes, 0)

    def along_x(z, carry):
        t = images[0, z]
        gx[z] = (lanes(t, -2) - lanes(t, 2) + 8.0 * (lanes(t, 1) - lanes(t, -1))) * (1.0 / 12.0)
        return carry

    lax.fori_loop(0, 8, along_x, 0)
    sh[...] = dot(shifts[...].astype(F32).astype(BF16), spread[...])
    un[...] = split_left(nodes[...], wi[...], 3)
    wy = lax.broadcasted_iota(jnp.int32, (8, 128), 0).astype(F32) * 0.125

    def chunk(c, energy):
        at = pl.ds(pl.multiple_of(c * 128, 128), 128)
        for er in range(2):
            base = 8 + 8 * er

            def full(row):
                return jnp.broadcast_to(row, (8, 128))

            sz = full(sh[er : er + 1, at])
            sy = full(sh[2 + er : 3 + er, at])
            sx = full(sh[4 + er : 5 + er, at])
            x_low, x_up = sx < -0.5, sx > 0.5
            y_low, y_up = sy < -0.5, sy > 0.5
            z_low, z_up = sz < -0.5, sz > 0.5

            def in_plane(k):
                rows = []
                for dy in (-1, 0, 1):
                    a, b, d = (pad1[i, k, base + dy : base + dy + 8, at] for i in range(3))
                    rows.append(jnp.where(x_low, a, jnp.where(x_up, d, b)))
                return jnp.where(y_low, rows[0], jnp.where(y_up, rows[2], rows[1]))

            corner = []
            for comp in range(3):
                for zn in range(2):
                    i = (comp * 2 + zn) * 3 + er
                    first, second = full(un[i : i + 1, at]), full(un[i + 1 : i + 2, at])
                    corner.append(first + wy * (second - first))
            sums = [None] * 18
            sums_rhs = [None] * 6
            planes = [in_plane(0), in_plane(1)]
            for z in range(8):
                planes.append(in_plane(z + 2))
                warped = jnp.where(z_low, planes[z], jnp.where(z_up, planes[z + 2], planes[z + 1]))
                here = lambda k: pad0[k, base : base + 8, at]
                rows = lambda dy: pad0[z + 2, base + dy : base + dy + 8, at]
                g0 = (here(z) - here(z + 4) + 8.0 * (here(z + 3) - here(z + 1))) * (1.0 / 12.0)
                g1 = (rows(-2) - rows(2) + 8.0 * (rows(1) - rows(-1))) * (1.0 / 12.0)
                g2 = gx[z, base - 8 : base, at]
                g = (g0, g1, g2)
                w = z / 8.0
                total = None
                for comp in range(3):
                    moved = corner[2 * comp] + w * (corner[2 * comp + 1] - corner[2 * comp])
                    term = g[comp] * moved
                    total = term if total is None else total + term
                mis = here(z + 2) - warped - total
                mismatch[z, base - 8 : base, at] = mis

                def add(store, i, weight, value):
                    if weight:
                        term = value if weight == 1.0 else weight * value
                        store[i] = term if store[i] is None else store[i] + term

                for ab, (a, b) in enumerate(PAIRS):
                    prod = g[a] * g[b]
                    if a == b:
                        energy = energy + prod
                    for zt, weight in enumerate(((1 - w) * (1 - w), w * (1 - w), w * w)):
                        add(sums, zt * 6 + ab, weight, prod)
                for comp in range(3):
                    prod = g[comp] * mis
                    for zt, weight in enumerate((1 - w, w)):
                        add(sums_rhs, zt * 3 + comp, weight, prod)
            for i in range(18):
                r = (i * 2 + er) * 8
                acc[r : r + 8, at] = sums[i]
            for i in range(6):
                r = (i * 2 + er) * 8
                acc_rhs[r : r + 8, at] = sums_rhs[i]
        return energy

    energy = lax.fori_loop(0, NCHUNK, chunk, jnp.zeros((8, 128), F32))
    by_x = split_left(acc[...], wq[...])
    by_x_rhs = split_left(acc_rhs[...], wl[...])
    by_y = split_right(ly[...], by_x)
    by_y_rhs = split_right(ry[...], by_x_rhs)
    for i, out in enumerate((own, to_slab, to_plane, to_both)):
        out[0:48, :] = by_y[48 * i : 48 * i + 48, 0:128]
        out[48:96, :] = by_y[48 * i : 48 * i + 48, 128:256]
        out[96:112, :] = jnp.zeros((16, 128), F32)
        out[96:102, :] = by_y_rhs[8 * i : 8 * i + 6, :]
    for yl in range(2):
        for comp in range(3):
            r = U_ROW + yl * 3 + comp
            i = comp * 6 + yl
            own[r : r + 1, :] = nodes[i : i + 1, :]
    own[ENERGY_ROW : ENERGY_ROW + 1, :] = jnp.sum(energy, axis=0, keepdims=True)


def local_part(images, zlo, zhi, ylo, yhi, shifts, nodes):
    vmem = pl.BlockSpec(memory_space=pltpu.VMEM)
    message = jax.ShapeDtypeStruct((ROWS, 128), F32)
    constants = build_constants()
    return pl.pallas_call(
        local_kernel,
        out_shape=(jax.ShapeDtypeStruct((8, 16, 1024), F32),) + (message,) * 4,
        in_specs=[vmem] * 13,
        out_specs=(vmem,) * 5,
        scratch_shapes=[
            pltpu.VMEM((12, 32, 1024), F32),
            pltpu.VMEM((3, 10, 32, 1024), F32),
            pltpu.VMEM((8, 16, 1024), F32),
            pltpu.VMEM((8, 1024), F32),
            pltpu.VMEM((24, 1024), F32),
            pltpu.VMEM((288, 1024), F32),
            pltpu.VMEM((96, 1024), F32),
        ],
        compiler_params=pltpu.CompilerParams(vmem_limit_bytes=40 << 20),
        name="local_part",
    )(images, zlo, zhi, ylo, yhi, shifts, nodes, *constants)


def solve_kernel(*refs):
    place, nodes = refs[0], refs[1]
    pieces = refs[2:14]
    out = refs[14]
    data, var, high, vec_x, vec_r, vec_p, vec_y = refs[15:]
    slab, plane = place[0], place[1]
    x_me, y_me = slab // 2, (slab % 2) * 2 + (plane // 2) % 2
    z_me, core = plane // 4, plane % 2

    def arrange(j, carry):
        for source in range(2):
            k = core if source == 0 else 1 - core
            first, second = 1 + 2 * k, 3 - 2 * k
            bits = [(j >> i) & 1 for i in range(5)]
            for color in range(3):
                start, count = COLORS[color]
                order = [(color + i) % 3 for i in range(3)]
                for half in range(2):
                    delta = [bits[0] * first, bits[1] * first, bits[2] * first]
                    delta[order[0]] = delta[order[0]] ^ (bits[3] * second)
                    delta[order[1]] = delta[order[1]] ^ (bits[4] * second)
                    if half:
                        delta[order[2]] = delta[order[2]] ^ second
                    x, y, z = x_me ^ delta[0], y_me ^ delta[1], z_me ^ delta[2]
                    device = (x * 2 + (y >> 1)) * 16 + z * 4 + (y & 1) * 2 + k
                    piece = pieces[(source * 2 + half) * 3 + color]
                    for t in range(count // 8):
                        r = (start + 8 * t) * STRIDE
                        data[pl.ds(r + device, 8, stride=STRIDE), :] = piece[j, 8 * t : 8 * t + 8, :]
        return carry

    lax.fori_loop(0, 32, arrange, 0)

    def field(r):
        return data[r * STRIDE : r * STRIDE + 128, :]

    total = jnp.sum(jnp.sum(field(ENERGY_ROW), axis=0, keepdims=True), axis=1, keepdims=True)
    penalty = reg_weight / (64.0 * 256.0 * 1024.0) * total

    def row_of(tx, tz, yk, ab):
        return ((tx * 2 + tz) * 4 + yk) * 6 + ab

    for ab in (0, 3, 5):
        for yk in range(2):
            for tx, tz, y_kind, weight in (
                (0, 0, yk, 6.0), (0, 0, 2 + yk, -1.0), (0, 1, yk, -1.0), (1, 0, yk, -1.0)
            ):
                r = row_of(tx, tz, y_kind, ab) * STRIDE
                data[r : r + 128, :] = data[r : r + 128, :] + weight * penalty

    lane = lax.broadcasted_iota(jnp.int32, (128, 128), 1)
    row = lax.broadcasted_iota(jnp.int32, (128, 128), 0)
    in_plane = row % 16

    def x_next(v):
        return jnp.where(lane < 127, pltpu.roll(v, 127, 1), 0.0)

    def x_prev(v):
        return jnp.where(lane > 0, pltpu.roll(v, 1, 1), 0.0)

    def p_next(v):
        return jnp.where(in_plane < 15, pltpu.roll(v, 127, 0), 0.0)

    def p_prev(v):
        return jnp.where(in_plane > 0, pltpu.roll(v, 1, 0), 0.0)

    zero = jnp.zeros((16, 128), F32)

    def z_next(v):
        return jnp.concatenate([v[16:], zero], axis=0)

    def z_prev(v):
        return jnp.concatenate([zero, v[:112]], axis=0)

    for comp in range(3):
        u = [field(U_ROW + yl * 3 + comp) for yl in range(2)]
        for yl in range(2):
            v = u[yl]
            beside = z_next(v) + z_prev(v) + x_next(v) + x_prev(v)
            beside = beside + (u[1] + p_prev(u[1]) if yl == 0 else u[0] + p_next(u[0]))
            rhs = field(RHS_ROW + yl * 3 + comp) - penalty * (6.0 * v - beside)
            i = comp * 2 + yl
            vec_r[i] = rhs
            vec_p[i] = rhs
            vec_x[i] = jnp.zeros((128, 128), F32)

    def norm():
        value = None
        for i in range(6):
            term = vec_r[i] * vec_r[i]
            value = term if value is None else value + term
        return jnp.sum(jnp.sum(value, axis=0, keepdims=True), axis=1, keepdims=True)

    var[8] = jnp.zeros((18, 16, 128), F32)
    lane16 = lax.broadcasted_iota(jnp.int32, (16, 128), 1)
    row16 = lax.broadcasted_iota(jnp.int32, (16, 128), 0)

    def multiply(z, energy):
        here = pl.ds(pl.multiple_of(z * 16, 16), 16)
        values = [
            [var[z + dz, i] for i in range(18)] for dz in range(2)
        ]

        def mat(tx, tz, yk, ab):
            start = row_of(tx, tz, yk, ab) * STRIDE
            return data[pl.ds(pl.multiple_of(start + z * 16, 8), 16), :]

        def accumulate(z_out, y_out, x_out):
            sums = [high[3 * (y_out * 2 + x_out) + a] if z_out == 0 else None for a in range(3)]
            for tz in range(2):
                if tz == 0 and z_out == 1:
                    continue
                z_in = 0 if tz == 0 else 1 - z_out
                for tx in range(2):
                    if tx == 0 and x_out == 1:
                        continue
                    x_in = 0 if tx == 0 else 1 - x_out
                    if y_out == 0:
                        kinds = ((0, 0), (2, 1))
                    elif y_out == 1:
                        kinds = ((1, 1), (2, 0), (3, 2))
                    else:
                        kinds = ((3, 1),)
                    for yk, y_in in kinds:
                        m = [mat(tx, tz, yk, ab) for ab in range(6)]
                        v = [values[z_in][(b * 3 + y_in) * 2 + x_in] for b in range(3)]
                        for a in range(3):
                            term = m[AB[a][0]] * v[0] + m[AB[a][1]] * v[1] + m[AB[a][2]] * v[2]
                            sums[a] = term if sums[a] is None else sums[a] + term
            return sums

        lows = [[accumulate(0, y_out, x_out) for x_out in range(2)] for y_out in range(3)]
        for a in range(3):
            parts = [
                lows[y][0][a] + jnp.where(lane16 > 0, pltpu.roll(lows[y][1][a], 1, 1), 0.0)
                for y in range(3)
            ]
            down = jnp.where(row16 > 0, pltpu.roll(parts[2], 1, 0), 0.0)
            result = (parts[0] + down, parts[1])
            for yl in range(2):
                vec_y[a * 2 + yl, here, :] = result[yl]
                energy = energy + result[yl] * values[0][(a * 3 + yl) * 2]
        for y_out in range(3):
            for x_out in range(2):
                sums = accumulate(1, y_out, x_out)
                for a in range(3):
                    high[3 * (y_out * 2 + x_out) + a] = sums[a]
        return energy

    def sweep(step, norm_now):
        for comp in range(3):
            own = [vec_p[comp * 2 + yl] for yl in range(2)]
            for y_kind, v in enumerate((own[0], own[1], p_next(own[0]))):
                i = (comp * 3 + y_kind) * 2
                var[0:8, i] = v.reshape(8, 16, 128)
                var[0:8, i + 1] = x_next(v).reshape(8, 16, 128)
        high[...] = jnp.zeros((18, 16, 128), F32)
        energy = lax.fori_loop(0, 8, multiply, jnp.zeros((16, 128), F32))
        curvature = jnp.sum(jnp.sum(energy, axis=0, keepdims=True), axis=1, keepdims=True)
        size = norm_now / curvature
        for i in range(6):
            vec_x[i] = vec_x[i] + size * vec_p[i]
            vec_r[i] = vec_r[i] - size * vec_y[i]
        norm_next = norm()
        ratio = norm_next / norm_now
        for i in range(6):
            vec_p[i] = vec_r[i] + ratio * vec_p[i]
        return norm_next

    lax.fori_loop(0, ITERS, sweep, norm())
    mine = slab * 16 + plane
    for comp in range(3):
        for yl in range(2):
            i = comp * 6 + yl
            out[comp * 2 + yl : comp * 2 + yl + 1, :] = (
                nodes[i : i + 1, :] + vec_x[comp * 2 + yl, pl.ds(mine, 1), :]
            )


def solve_part(place, nodes, pieces):
    vmem = pl.BlockSpec(memory_space=pltpu.VMEM)
    return pl.pallas_call(
        solve_kernel,
        out_shape=jax.ShapeDtypeStruct((6, 128), F32),
        in_specs=[pl.BlockSpec(memory_space=pltpu.SMEM)] + [vmem] * 13,
        out_specs=vmem,
        scratch_shapes=[
            pltpu.VMEM((ROWS * STRIDE, 128), F32),
            pltpu.VMEM((9, 18, 16, 128), F32),
            pltpu.VMEM((18, 16, 128), F32),
        ]
        + [pltpu.VMEM((6, 128, 128), F32)] * 4,
        compiler_params=pltpu.CompilerParams(vmem_limit_bytes=48 << 20),
        name="solve_part",
    )(place, nodes, *pieces)


def coordinates(device):
    slab, plane = divmod(device, 16)
    x, y_hi = divmod(slab, 2)
    z, rest = divmod(plane, 4)
    y_lo, core = divmod(rest, 2)
    return [x, y_hi * 2 + y_lo, z, core]


def device_of(x, y, z, core):
    return (x * 2 + y // 2) * 16 + z * 4 + (y % 2) * 2 + core


def exchange(value, axis, second):
    pairs = []
    for device in range(128):
        at = coordinates(device)
        if axis == 3:
            at[3] = 1 - at[3]
        else:
            at[axis] ^= 3 if (at[3] == 1) != second else 1
        pairs.append((device, device_of(*at)))
    return lax.ppermute(value, AXES, pairs)


def shifted(value, slab_step, plane_step):
    pairs = []
    for slab in range(8 - slab_step):
        for plane in range(16 - plane_step):
            pairs.append((slab * 16 + plane, (slab + slab_step) * 16 + plane + plane_step))
    return lax.ppermute(value, AXES, pairs)


def neighbours(forward, backward, axis):
    count = lax.axis_size(axis)
    up = [(i, i + 1) for i in range(count - 1)]
    down = [(i + 1, i) for i in range(count - 1)]
    return lax.ppermute(forward, axis, up), lax.ppermute(backward, axis, down)


def body(images, shifts, initial_displacement):
    ref, moving = images[0], images[1]
    own_nodes = initial_displacement.reshape(6, 128)

    def wide(rows):
        return jnp.pad(rows.reshape(1, 768), ((0, 0), (0, 256)))

    zlo, zhi = neighbours(
        jnp.concatenate([ref[6:8].reshape(32, 1024), moving[7]], 0),
        jnp.concatenate([ref[0:2].reshape(32, 1024), moving[0], wide(own_nodes)], 0),
        "slab",
    )
    above = zhi[48, :768].reshape(3, 2, 128)
    layers = jnp.stack([initial_displacement[:, 0], above], 1)
    ylo, yhi = neighbours(
        jnp.concatenate(
            [ref[:, 14:16].reshape(16, 1024), zlo[47:48], moving[:, 15], zhi[47:48]], 0
        ),
        jnp.concatenate(
            [
                ref[:, 0:2].reshape(16, 1024),
                zlo[32:33],
                moving[:, 0],
                zhi[32:33],
                wide(layers[:, :, 0]),
            ],
            0,
        ),
        "plane",
    )
    beyond = yhi[26, :768].reshape(3, 2, 1, 128)
    nodes = jnp.concatenate([layers, beyond], 2).reshape(18, 128)
    nodes = jnp.pad(nodes, ((0, 6), (0, 0)))
    elements = jnp.pad(shifts.reshape(6, 128), ((0, 2), (0, 0)))
    mismatch, own, to_slab, to_plane, to_both = local_part(
        images, zlo, zhi, ylo, yhi, elements, nodes
    )
    payload = own + shifted(to_slab, 1, 0) + shifted(to_plane, 0, 1) + shifted(to_both, 1, 1)
    blocks = payload[None]
    for axis in range(3):
        blocks = jnp.concatenate([blocks, exchange(blocks, axis, False)], 0)
    parts = [blocks[:, start : start + count] for start, count in COLORS]
    for turn in range(2):
        parts = [
            jnp.concatenate([part, exchange(part, (color + turn) % 3, True)], 0)
            for color, part in enumerate(parts)
        ]
    last = [exchange(part, (color + 2) % 3, True) for color, part in enumerate(parts)]
    pieces = parts + last
    pieces = pieces + [exchange(piece, 3, False) for piece in pieces]
    place = jnp.stack([lax.axis_index("slab"), lax.axis_index("plane")]).astype(jnp.int32)
    result = solve_part(place, nodes, pieces)
    return result.reshape(3, 1, 2, 128), mismatch


def solution(mesh):
    in_specs = (
        P(None, "slab", "plane", None),
        P(None, "slab", "plane", None),
        P(None, "slab", "plane", None),
    )
    out_specs = (P(None, "slab", "plane", None), P("slab", "plane", None))
    return jax.shard_map(body, mesh=mesh, in_specs=in_specs, out_specs=out_specs, check_vma=False)
```

time: 1270 us -> 134 us (0.11)
  blocking collectives: 783 us -> 0 us
  other arithmetic: 139 us -> 1.79 us
  local copies, waits for them, and re-layouts: 140 us -> 5.68 us
  starting transfers between devices: 163 us -> 64 us
  Pallas kernels: 0 us -> 31 us
  between operations: 18.8 us -> 1 us
  waiting for transfers between devices: 13.6 us -> 30.5 us
    psum x12 -> x0, blocking collectives: 783 us -> none  [the longest x6 384 us: residual_norm(): return lax.psum(jnp.sum(residual * residual * counted), ('slab', 'plane'))]
    ppermute x46 -> x25, starting transfers between devices: 163 us -> 64 us  [the longest x18 38.4 us: exchange(): return lax.ppermute(value, AXES, pairs)]
    sub x2 -> x0, other arithmetic: 59.9 us -> none  [the longest x1 59.1 us: body(): mismatch = images[0] - warped - jnp.sum(grads * moved, 0)]
    eq x54 -> x0, local copies, waits for them, and re-layouts: 40.6 us -> none  [warp_image(): result = jnp.where(codes == candidate, piece, result)]
    pallas_call x0 -> x2, Pallas kernels: none -> 31 us  [the longest x1 23.4 us: solve_part(): pl.pallas_call(solve_kernel, out_shape=jax.ShapeDtypeStruct((6, 128), F32...]
    reduce_sum x40 -> x0, other arithmetic: 23 us -> none  [the longest x7 9.63 us: collapse_width(): upper = jnp.sum(blocks * weights, -1)]
    unnamed x180 -> x23, local copies, waits for them, and re-layouts: 24.2 us -> 2.68 us
    add x26 -> x0, other arithmetic: 19.5 us -> none  [the longest x7 18 us: collapse_width(): lower + jnp.concatenate([jnp.zeros_like(upper[..., :1]), upper[..., :-1]]...]
  transfers between devices with their start and end apart: 46 -> 25, of which waited for: 18 -> 12; matrix products, arithmetic and copies ran while one was open for 17% -> 1% of each run, Pallas kernels for 0% -> 0%
where the time goes in v1:
time: 134 us
  starting transfers between devices  64 us (48%)
  Pallas kernels  31 us (23%)
  waiting for transfers between devices  30.5 us (23%)
  local copies, waits for them, and re-layouts  5.68 us (4%)
  other arithmetic  1.79 us (1%)
    ppermute x18, starting transfers between devices, exchange(): return lax.ppermute(value, AXES, pairs)  38.4 us
    pallas_call x1, Pallas kernels, solve_part(): pl.pallas_call(solve_kernel, out_shape=jax.ShapeDtypeStruct((6, 128), F32...  23.4 us
    ppermute x18, waiting for transfers between devices, exchange(): return lax.ppermute(value, AXES, pairs)  20.6 us
    ppermute x4, starting transfers between devices, neighbours(): return (lax.ppermute(forward, axis, up), lax.ppermute(backward, axis, down))  13.2 us
    ppermute x3, starting transfers between devices, shifted(): return lax.ppermute(value, AXES, pairs)  12.4 us
    ppermute x4, waiting for transfers between devices, neighbours(): return (lax.ppermute(forward, axis, up), lax.ppermute(backward, axis, down))  8.65 us
    pallas_call x1, Pallas kernels, local_part(): pl.pallas_call(local_kernel, out_shape=(jax.ShapeDtypeStruct((8, 16, 1024...  7.63 us
  transfers between devices with their start and end apart: 25, of which 12 were waited for; matrix products, arithmetic and copies ran while one was open for 1% of the time, Pallas kernels for 0%

profile of v1, /device:TPU:1, one launch (start us, length us, event | category | flops | bytes accessed | tf_op | source)
XLA Modules:
  0.0 134.0 jit_solution(7484270013822792777)
XLA Ops:
  0.6 1.1 fusion
  1.7 0.9 slice_bitcast_fusion.2
  2.6 0.7 select_maximum_fusion
  3.3 1.3 collective-permute-start
  4.6 0.7 pad_maximum_fusion.8
  5.3 6.3 %collective-permute-start.1 = (f32[48,1024]{1,0:T(8,128)}, f32[48,1024]{1,0:T(8,128)S(1)}, u32[]{:S(2)}, u32[]{:S(2)}) collective-permute-start(f32[48,1024]{1,0:T(8,128)} %pad_maximum_fusion.8), channel_id=1, source_target_pairs={{0,16},{16,32},{32,48},{48,64},{64,80},{80,96},{96,112},{1,17},{17... | collective-permute-start | bytes 589832 | tf_op jit(solution)/shard_map/ppermute | solution.py:496
  11.7 0.3 copy.21
  12.2 0.5 copy-done.10
  12.7 6.8 %collective-permute-done.1.zlo = f32[48,1024]{1,0:T(8,128)S(1)} collective-permute-done((f32[48,1024]{1,0:T(8,128)}, f32[48,1024]{1,0:T(8,128)S(1)}, u32[]{:S(2)}, u32[]{:S(2)}) %collective-permute-start.1) | collective-permute-done | bytes 196640 | tf_op jit(solution)/shard_map/ppermute | solution.py:496
  19.6 0.2 concatenate.49
  19.7 2.4 %collective-permute-start.2 = (f32[27,1024]{1,0:T(8,128)S(1)}, f32[27,1024]{1,0:T(8,128)S(1)}, u32[]{:S(2)}, u32[]{:S(2)}) collective-permute-start(f32[27,1024]{1,0:T(8,128)S(1)} %concatenate.49), channel_id=1, source_target_pairs={{1,0},{2,1},{3,2},{4,3},{5,4},{6,5},{7,6},{8,7},{9,8},{10,9},{11,1... | collective-permute-start | bytes 331784 | tf_op jit(solution)/shard_map/ppermute | solution.py:496
  22.2 3.3 %collective-permute-start.3 = (f32[26,1024]{1,0:T(8,128)S(1)}, f32[26,1024]{1,0:T(8,128)S(1)}, u32[]{:S(2)}, u32[]{:S(2)}) collective-permute-start(f32[26,1024]{1,0:T(8,128)S(1)} %pad_maximum_fusion.10), channel_id=1, source_target_pairs={{0,1},{1,2},{2,3},{3,4},{4,5},{5,6},{6,7},{7,8},{8,9},{9,10},{10,1... | collective-permute-start | bytes 319496 | tf_op jit(solution)/shard_map/ppermute | solution.py:496
  25.5 0.5 collective-permute-done.2.yhi
  26.1 1.3 collective-permute-done.3.ylo
  27.4 7.6 %local_part.1 = (f32[8,16,1024]{2,1,0:T(8,128)}, f32[112,128]{1,0:T(8,128)S(1)}, f32[112,128]{1,0:T(8,128)S(1)}, f32[112,128]{1,0:T(8,128)S(1)}, f32[112,128]{1,0:T(8,128)S(1)}) custom-call(f32[2,8,16,1024]{3,2,1,0:T(8,128)S(1)} %copy-done, f32[48,1024]{1,0:T(8,128)S(1)} %collective-permute-done.1.zlo, f32[49,1024]{1,0:T(8,128)S(1)} %collective-permute-done.zhi, ...), custom_call_target="tpu_custom_call" | custom-call | tf_op jit(solution)/shard_map/local_part/pallas_call | solution.py:244
  35.1 5.5 %collective-permute-start.4 = (f32[112,128]{1,0:T(8,128)S(1)}, f32[112,128]{1,0:T(8,128)S(1)}, u32[]{:S(2)}, u32[]{:S(2)}) collective-permute-start(f32[112,128]{1,0:T(8,128)S(1)} %get-tuple-element.8), channel_id=1, source_target_pairs={{0,16},{1,17},{2,18},{3,19},{4,20},{5,21},{6,22},{7,23},{8,24},{9,... | collective-permute-start | bytes 172040 | tf_op jit(solution)/shard_map/ppermute | solution.py:489
  40.6 4.0 %collective-permute-start.5 = (f32[112,128]{1,0:T(8,128)S(1)}, f32[112,128]{1,0:T(8,128)S(1)}, u32[]{:S(2)}, u32[]{:S(2)}) collective-permute-start(f32[112,128]{1,0:T(8,128)S(1)} %get-tuple-element.9), channel_id=1, source_target_pairs={{0,1},{1,2},{2,3},{3,4},{4,5},{5,6},{6,7},{7,8},{8,9},{9,10},{10,1... | collective-permute-start | bytes 172040 | tf_op jit(solution)/shard_map/ppermute | solution.py:489
  44.6 2.8 %collective-permute-start.6 = (f32[112,128]{1,0:T(8,128)S(1)}, f32[112,128]{1,0:T(8,128)S(1)}, u32[]{:S(2)}, u32[]{:S(2)}) collective-permute-start(f32[112,128]{1,0:T(8,128)S(1)} %get-tuple-element.10), channel_id=1, source_target_pairs={{0,17},{1,18},{2,19},{3,20},{4,21},{5,22},{6,23},{7,24},{8,25},{9,... | collective-permute-start | bytes 172040 | tf_op jit(solution)/shard_map/ppermute | solution.py:489
  47.5 1.2 collective-permute-done.6
  48.7 4.4 %collective-permute-start.7 = (f32[1,112,128]{2,1,0:T(8,128)S(1)}, f32[1,112,128]{2,1,0:T(8,128)S(1)}, u32[]{:S(2)}, u32[]{:S(2)}) collective-permute-start(f32[1,112,128]{2,1,0:T(8,128)S(1)} %add_bitcast_fusion), channel_id=1, source_target_pairs={{0,32},{1,97},{2,34},{3,99},{4,36},{5,101},{6,38},{7,103},{8,40},{... | collective-permute-start | bytes 172040 | tf_op jit(solution)/shard_map/ppermute | solution.py:481
  53.1 1.6 %collective-permute-done.7 = f32[1,112,128]{2,1,0:T(8,128)S(1)} collective-permute-done((f32[1,112,128]{2,1,0:T(8,128)S(1)}, f32[1,112,128]{2,1,0:T(8,128)S(1)}, u32[]{:S(2)}, u32[]{:S(2)}) %collective-permute-start.7) | collective-permute-done | bytes 57376 | tf_op jit(solution)/shard_map/ppermute | solution.py:481
  54.6 4.9 %collective-permute-start.8 = (f32[2,112,128]{2,1,0:T(8,128)S(1)}, f32[2,112,128]{2,1,0:T(8,128)S(1)}, u32[]{:S(2)}, u32[]{:S(2)}) collective-permute-start(f32[2,112,128]{2,1,0:T(8,128)S(1)} %pad_maximum_fusion.11), channel_id=1, source_target_pairs={{0,2},{1,19},{2,0},{3,17},{4,6},{5,23},{6,4},{7,21},{8,10},{9,27},... | collective-permute-start | bytes 344072 | tf_op jit(solution)/shard_map/ppermute | solution.py:481
  59.6 2.2 %collective-permute-done.8 = f32[2,112,128]{2,1,0:T(8,128)S(1)} collective-permute-done((f32[2,112,128]{2,1,0:T(8,128)S(1)}, f32[2,112,128]{2,1,0:T(8,128)S(1)}, u32[]{:S(2)}, u32[]{:S(2)}) %collective-permute-start.8) | collective-permute-done | bytes 114720 | tf_op jit(solution)/shard_map/ppermute | solution.py:481
  61.8 2.4 %collective-permute-start.9 = (f32[4,112,128]{2,1,0:T(8,128)S(1)}, f32[4,112,128]{2,1,0:T(8,128)S(1)}, u32[]{:S(2)}, u32[]{:S(2)}) collective-permute-start(f32[4,112,128]{2,1,0:T(8,128)S(1)} %pad_maximum_fusion.7), channel_id=1, source_target_pairs={{0,4},{1,13},{2,6},{3,15},{4,0},{5,9},{6,2},{7,11},{8,12},{9,5},{1... | collective-permute-start | bytes 688136 | tf_op jit(solution)/shard_map/ppermute | solution.py:481
  64.2 3.7 %collective-permute-done.9 = f32[4,112,128]{2,1,0:T(8,128)S(1)} collective-permute-done((f32[4,112,128]{2,1,0:T(8,128)S(1)}, f32[4,112,128]{2,1,0:T(8,128)S(1)}, u32[]{:S(2)}, u32[]{:S(2)}) %collective-permute-start.9) | collective-permute-done | bytes 229408 | tf_op jit(solution)/shard_map/ppermute | solution.py:481
  68.0 0.1 collective-permute-start.12
  68.1 2.2 %collective-permute-start.10 = (f32[8,40,128]{2,1,0:T(8,128)S(1)}, f32[8,40,128]{2,1,0:T(8,128)S(1)}, u32[]{:S(2)}, u32[]{:S(2)}) collective-permute-start(f32[8,40,128]{2,1,0:T(8,128)S(1)} %get-tuple-element.27), channel_id=1, source_target_pairs={{0,96},{1,33},{2,98},{3,35},{4,100},{5,37},{6,102},{7,39},{8,104},... | collective-permute-start | bytes 491528 | tf_op jit(solution)/shard_map/ppermute | solution.py:481
  70.3 1.9 %collective-permute-done.12 = f32[8,40,128]{2,1,0:T(8,128)S(1)} collective-permute-done((f32[8,40,128]{2,1,0:T(8,128)S(1)}, f32[8,40,128]{2,1,0:T(8,128)S(1)}, u32[]{:S(2)}, u32[]{:S(2)}) %collective-permute-start.12) | collective-permute-done | bytes 163872 | tf_op jit(solution)/shard_map/ppermute | solution.py:481
  72.3 0.8 collective-permute-start.13
  73.1 0.8 collective-permute-start.14
  74.0 0.4 collective-permute-start.11
  74.4 5.4 %collective-permute-done.14 = f32[8,32,128]{2,1,0:T(8,128)S(1)} collective-permute-done((f32[8,32,128]{2,1,0:T(8,128)S(1)}, f32[8,32,128]{2,1,0:T(8,128)S(1)}, u32[]{:S(2)}, u32[]{:S(2)}) %collective-permute-start.14) | collective-permute-done | bytes 131104 | tf_op jit(solution)/shard_map/ppermute | solution.py:481
  79.7 1.2 collective-permute-start.15
  81.0 0.4 collective-permute-start.17
  81.5 1.1 collective-permute-start.16
  82.6 2.8 %collective-permute-done.15 = f32[16,32,128]{2,1,0:T(8,128)S(1)} collective-permute-done((f32[16,32,128]{2,1,0:T(8,128)S(1)}, f32[16,32,128]{2,1,0:T(8,128)S(1)}, u32[]{:S(2)}, u32[]{:S(2)}) %collective-permute-start.15) | collective-permute-done | bytes 262176 | tf_op jit(solution)/shard_map/ppermute | solution.py:481
  85.4 1.1 collective-permute-start.18
  86.5 8.8 %collective-permute-start.21 = (f32[32,32,128]{2,1,0:T(8,128)S(1)}, f32[32,32,128]{2,1,0:T(8,128)S(1)}, u32[]{:S(2)}, u32[]{:S(2)}) collective-permute-start(f32[32,32,128]{2,1,0:T(8,128)S(1)} %pad_maximum_fusion.2.refs_4_), channel_id=1, source_target_pairs={{0,1},{1,0},{2,3},{3,2},{4,5},{5,4},{6,7},{7,6},{8,9},{9,8},{10,11... | collective-permute-start | bytes 1572872 | tf_op jit(solution)/shard_map/ppermute | solution.py:481
  95.3 9.2 %collective-permute-start.19 = (f32[32,40,128]{2,1,0:T(8,128)S(1)}, f32[32,40,128]{2,1,0:T(8,128)}, u32[]{:S(2)}, u32[]{:S(2)}) collective-permute-start(f32[32,40,128]{2,1,0:T(8,128)S(1)} %pad_maximum_fusion.refs_2_), channel_id=1, source_target_pairs={{0,1},{1,0},{2,3},{3,2},{4,5},{5,4},{6,7},{7,6},{8,9},{9,8},{10,11... | collective-permute-start | bytes 1966088 | tf_op jit(solution)/shard_map/ppermute | solution.py:481
  104.5 0.5 collective-permute-start.22
  105.0 0.8 copy-done.2
  105.8 0.1 collective-permute-start.24
  105.9 0.1 pad_add_fusion.refs_0_
  105.9 0.4 collective-permute-done.19.refs_8_
  106.3 2.6 %collective-permute-done.24.refs_13_ = f32[32,32,128]{2,1,0:T(8,128)} collective-permute-done((f32[32,32,128]{2,1,0:T(8,128)}, f32[32,32,128]{2,1,0:T(8,128)}, u32[]{:S(2)}, u32[]{:S(2)}) %collective-permute-start.24) | collective-permute-done | bytes 524320 | tf_op jit(solution)/shard_map/ppermute | solution.py:481
  109.0 1.0 copy-done.3
  110.0 23.4 %solve_part.1 = f32[6,128]{1,0:T(8,128)S(1)} custom-call(s32[2]{0:T(128)S(1)} %pad_add_fusion.refs_0_, f32[24,128]{1,0:T(8,128)S(1)} %pad.17.nodes.refs_1_, f32[32,40,128]{2,1,0:T(8,128)S(1)} %pad_maximum_fusion.refs_2_, f32[32,40,128]{2,1,0:T(8,128)S(1)} %pad_maximum_fusion.1.refs_3_, f32[32,32,128]{2,1,0:T(8,128)S(1)} %pad_maximum_fusion.2.refs_4_, ...), custom_call_target="tpu_custom_call" | custom-call | tf_op jit(solution)/shard_map/solve_part/pallas_call | solution.py:444
  133.4 0.6 reshape.39
  (63 shorter events, 0.7 us)
Async XLA Ops:
  0.6 10.9 %copy-start = (f32[2,8,16,1024]{3,2,1,0:T(8,128)S(1)}, f32[2,8,16,1024]{3,2,1,0:T(8,128)}, u32[]{:S(2)}) copy-start(f32[2,8,16,1024]{3,2,1,0:T(8,128)} %images.1) | copy-start | bytes 3145732
  3.3 16.2 %collective-permute-start = (f32[49,1024]{1,0:T(8,128)S(1)}, f32[49,1024]{1,0:T(8,128)S(1)}, u32[]{:S(2)}, u32[]{:S(2)}) collective-permute-start(f32[49,1024]{1,0:T(8,128)S(1)} %select_maximum_fusion), channel_id=1, source_target_pairs={{16,0},{32,16},{48,32},{64,48},{80,64},{96,80},{112,96},{17,1},{33... | collective-permute-start | bytes 602120 | tf_op jit(solution)/shard_map/ppermute | solution.py:496
  5.3 14.2 %collective-permute-start.1 = (f32[48,1024]{1,0:T(8,128)}, f32[48,1024]{1,0:T(8,128)S(1)}, u32[]{:S(2)}, u32[]{:S(2)}) collective-permute-start(f32[48,1024]{1,0:T(8,128)} %pad_maximum_fusion.8), channel_id=1, source_target_pairs={{0,16},{16,32},{32,48},{48,64},{64,80},{80,96},{96,112},{1,17},{17... | collective-permute-start | bytes 589832 | tf_op jit(solution)/shard_map/ppermute | solution.py:496
  11.7 15.7 %copy-start.6 = (bf16[128,1024]{1,0:T(8,128)(2,1)S(1)}, bf16[128,1024]{1,0:T(8,128)(2,1)}, u32[]{:S(2)}) copy-start(bf16[128,1024]{1,0:T(8,128)(2,1)} %constant.44.spread) | copy-start | bytes 786436
  12.0 0.7 copy-start.10
  12.0 7.5 %copy-start.9 = (f32[3,1,2,128]{3,2,1,0:T(2,128)S(1)}, f32[3,1,2,128]{3,2,1,0:T(2,128)}, u32[]{:S(2)}) copy-start(f32[3,1,2,128]{3,2,1,0:T(2,128)} %param.11) | copy-start | bytes 9220
  12.0 15.4 %copy-start.5 = (bf16[128,1024]{1,0:T(8,128)(2,1)S(1)}, bf16[128,1024]{1,0:T(8,128)(2,1)}, u32[]{:S(2)}) copy-start(bf16[128,1024]{1,0:T(8,128)(2,1)} %constant.43.wi) | copy-start | bytes 786436
  12.1 15.3 %copy-start.1 = (bf16[1024,256]{1,0:T(8,128)(2,1)S(1)}, bf16[1024,256]{1,0:T(8,128)(2,1)}, u32[]{:S(2)}) copy-start(bf16[1024,256]{1,0:T(8,128)(2,1)} %constant.41.wq) | copy-start | bytes 1572868
  19.6 7.8 %copy-start.4 = (bf16[1024,128]{1,0:T(8,128)(2,1)S(1)}, bf16[1024,128]{1,0:T(8,128)(2,1)}, u32[]{:S(2)}) copy-start(bf16[1024,128]{1,0:T(8,128)(2,1)} %constant.42.wl) | copy-start | bytes 786436
  19.7 6.3 %collective-permute-start.2 = (f32[27,1024]{1,0:T(8,128)S(1)}, f32[27,1024]{1,0:T(8,128)S(1)}, u32[]{:S(2)}, u32[]{:S(2)}) collective-permute-start(f32[27,1024]{1,0:T(8,128)S(1)} %concatenate.49), channel_id=1, source_target_pairs={{1,0},{2,1},{3,2},{4,3},{5,4},{6,5},{7,6},{8,7},{9,8},{10,9},{11,1... | collective-permute-start | bytes 331784 | tf_op jit(solution)/shard_map/ppermute | solution.py:496
  22.1 5.3 %copy-start.7 = (bf16[192,288]{1,0:T(8,128)(2,1)S(1)}, bf16[192,288]{1,0:T(8,128)(2,1)}, u32[]{:S(2)}) copy-start(bf16[192,288]{1,0:T(8,128)(2,1)} %constant.45.ly) | copy-start | bytes 331780
  22.2 5.2 %collective-permute-start.3 = (f32[26,1024]{1,0:T(8,128)S(1)}, f32[26,1024]{1,0:T(8,128)S(1)}, u32[]{:S(2)}, u32[]{:S(2)}) collective-permute-start(f32[26,1024]{1,0:T(8,128)S(1)} %pad_maximum_fusion.10), channel_id=1, source_target_pairs={{0,1},{1,2},{2,3},{3,4},{4,5},{5,6},{6,7},{7,8},{8,9},{9,10},{10,1... | collective-permute-start | bytes 319496 | tf_op jit(solution)/shard_map/ppermute | solution.py:496
  26.0 1.4 %copy-start.8 = (bf16[32,96]{1,0:T(8,128)(2,1)S(1)}, bf16[32,96]{1,0:T(8,128)(2,1)}, u32[]{:S(2)}) copy-start(bf16[32,96]{1,0:T(8,128)(2,1)} %constant.46.ry) | copy-start | bytes 18436
  35.1 12.4 %collective-permute-start.4 = (f32[112,128]{1,0:T(8,128)S(1)}, f32[112,128]{1,0:T(8,128)S(1)}, u32[]{:S(2)}, u32[]{:S(2)}) collective-permute-start(f32[112,128]{1,0:T(8,128)S(1)} %get-tuple-element.8), channel_id=1, source_target_pairs={{0,16},{1,17},{2,18},{3,19},{4,20},{5,21},{6,22},{7,23},{8,24},{9,... | collective-permute-start | bytes 172040 | tf_op jit(solution)/shard_map/ppermute | solution.py:489
  40.6 6.9 %collective-permute-start.5 = (f32[112,128]{1,0:T(8,128)S(1)}, f32[112,128]{1,0:T(8,128)S(1)}, u32[]{:S(2)}, u32[]{:S(2)}) collective-permute-start(f32[112,128]{1,0:T(8,128)S(1)} %get-tuple-element.9), channel_id=1, source_target_pairs={{0,1},{1,2},{2,3},{3,4},{4,5},{5,6},{6,7},{7,8},{8,9},{9,10},{10,1... | collective-permute-start | bytes 172040 | tf_op jit(solution)/shard_map/ppermute | solution.py:489
  44.6 4.1 %collective-permute-start.6 = (f32[112,128]{1,0:T(8,128)S(1)}, f32[112,128]{1,0:T(8,128)S(1)}, u32[]{:S(2)}, u32[]{:S(2)}) collective-permute-start(f32[112,128]{1,0:T(8,128)S(1)} %get-tuple-element.10), channel_id=1, source_target_pairs={{0,17},{1,18},{2,19},{3,20},{4,21},{5,22},{6,23},{7,24},{8,25},{9,... | collective-permute-start | bytes 172040 | tf_op jit(solution)/shard_map/ppermute | solution.py:489
  48.7 5.9 %collective-permute-start.7 = (f32[1,112,128]{2,1,0:T(8,128)S(1)}, f32[1,112,128]{2,1,0:T(8,128)S(1)}, u32[]{:S(2)}, u32[]{:S(2)}) collective-permute-start(f32[1,112,128]{2,1,0:T(8,128)S(1)} %add_bitcast_fusion), channel_id=1, source_target_pairs={{0,32},{1,97},{2,34},{3,99},{4,36},{5,101},{6,38},{7,103},{8,40},{... | collective-permute-start | bytes 172040 | tf_op jit(solution)/shard_map/ppermute | solution.py:481
  54.6 7.1 %collective-permute-start.8 = (f32[2,112,128]{2,1,0:T(8,128)S(1)}, f32[2,112,128]{2,1,0:T(8,128)S(1)}, u32[]{:S(2)}, u32[]{:S(2)}) collective-permute-start(f32[2,112,128]{2,1,0:T(8,128)S(1)} %pad_maximum_fusion.11), channel_id=1, source_target_pairs={{0,2},{1,19},{2,0},{3,17},{4,6},{5,23},{6,4},{7,21},{8,10},{9,27},... | collective-permute-start | bytes 344072 | tf_op jit(solution)/shard_map/ppermute | solution.py:481
  61.8 6.2 %collective-permute-start.9 = (f32[4,112,128]{2,1,0:T(8,128)S(1)}, f32[4,112,128]{2,1,0:T(8,128)S(1)}, u32[]{:S(2)}, u32[]{:S(2)}) collective-permute-start(f32[4,112,128]{2,1,0:T(8,128)S(1)} %pad_maximum_fusion.7), channel_id=1, source_target_pairs={{0,4},{1,13},{2,6},{3,15},{4,0},{5,9},{6,2},{7,11},{8,12},{9,5},{1... | collective-permute-start | bytes 688136 | tf_op jit(solution)/shard_map/ppermute | solution.py:481
  68.0 4.2 %collective-permute-start.12 = (f32[8,40,128]{2,1,0:T(8,128)S(1)}, f32[8,40,128]{2,1,0:T(8,128)S(1)}, u32[]{:S(2)}, u32[]{:S(2)}) collective-permute-start(f32[8,40,128]{2,1,0:T(8,128)S(1)} %get-tuple-element.26), channel_id=1, source_target_pairs={{0,18},{1,3},{2,16},{3,1},{4,22},{5,7},{6,20},{7,5},{8,26},{9,11},... | collective-permute-start | bytes 491528 | tf_op jit(solution)/shard_map/ppermute | solution.py:481
  68.1 5.8 %collective-permute-start.10 = (f32[8,40,128]{2,1,0:T(8,128)S(1)}, f32[8,40,128]{2,1,0:T(8,128)S(1)}, u32[]{:S(2)}, u32[]{:S(2)}) collective-permute-start(f32[8,40,128]{2,1,0:T(8,128)S(1)} %get-tuple-element.27), channel_id=1, source_target_pairs={{0,96},{1,33},{2,98},{3,35},{4,100},{5,37},{6,102},{7,39},{8,104},... | collective-permute-start | bytes 491528 | tf_op jit(solution)/shard_map/ppermute | solution.py:481
  72.3 8.6 %collective-permute-start.13 = (f32[16,40,128]{2,1,0:T(8,128)S(1)}, f32[16,40,128]{2,1,0:T(8,128)S(1)}, u32[]{:S(2)}, u32[]{:S(2)}) collective-permute-start(f32[16,40,128]{2,1,0:T(8,128)S(1)} %pad_maximum_fusion.5), channel_id=1, source_target_pairs={{0,12},{1,5},{2,14},{3,7},{4,8},{5,1},{6,10},{7,3},{8,4},{9,13},{1... | collective-permute-start | bytes 983048 | tf_op jit(solution)/shard_map/ppermute | solution.py:481
  73.1 6.6 %collective-permute-start.14 = (f32[8,32,128]{2,1,0:T(8,128)S(1)}, f32[8,32,128]{2,1,0:T(8,128)S(1)}, u32[]{:S(2)}, u32[]{:S(2)}) collective-permute-start(f32[8,32,128]{2,1,0:T(8,128)S(1)} %pad_maximum_fusion.9), channel_id=1, source_target_pairs={{0,12},{1,5},{2,14},{3,7},{4,8},{5,1},{6,10},{7,3},{8,4},{9,13},{1... | collective-permute-start | bytes 393224 | tf_op jit(solution)/shard_map/ppermute | solution.py:481
  74.0 7.4 %collective-permute-start.11 = (f32[16,40,128]{2,1,0:T(8,128)S(1)}, f32[16,40,128]{2,1,0:T(8,128)S(1)}, u32[]{:S(2)}, u32[]{:S(2)}) collective-permute-start(f32[16,40,128]{2,1,0:T(8,128)S(1)} %pad_maximum_fusion.4), channel_id=1, source_target_pairs={{0,18},{1,3},{2,16},{3,1},{4,22},{5,7},{6,20},{7,5},{8,26},{9,11},... | collective-permute-start | bytes 983048 | tf_op jit(solution)/shard_map/ppermute | solution.py:481
  79.7 5.6 %collective-permute-start.15 = (f32[16,32,128]{2,1,0:T(8,128)S(1)}, f32[16,32,128]{2,1,0:T(8,128)S(1)}, u32[]{:S(2)}, u32[]{:S(2)}) collective-permute-start(f32[16,32,128]{2,1,0:T(8,128)S(1)} %pad_maximum_fusion.6), channel_id=1, source_target_pairs={{0,96},{1,33},{2,98},{3,35},{4,100},{5,37},{6,102},{7,39},{8,104},... | collective-permute-start | bytes 786440 | tf_op jit(solution)/shard_map/ppermute | solution.py:481
  81.0 23.5 %collective-permute-start.17 = (f32[32,40,128]{2,1,0:T(8,128)S(1)}, f32[32,40,128]{2,1,0:T(8,128)S(1)}, u32[]{:S(2)}, u32[]{:S(2)}) collective-permute-start(f32[32,40,128]{2,1,0:T(8,128)S(1)} %pad_maximum_fusion.1.refs_3_), channel_id=1, source_target_pairs={{0,96},{1,33},{2,98},{3,35},{4,100},{5,37},{6,102},{7,39},{8,104},... | collective-permute-start | bytes 1966088 | tf_op jit(solution)/shard_map/ppermute | solution.py:481
  81.5 23.0 %collective-permute-start.16 = (f32[32,40,128]{2,1,0:T(8,128)S(1)}, f32[32,40,128]{2,1,0:T(8,128)S(1)}, u32[]{:S(2)}, u32[]{:S(2)}) collective-permute-start(f32[32,40,128]{2,1,0:T(8,128)S(1)} %pad_maximum_fusion.refs_2_), channel_id=1, source_target_pairs={{0,12},{1,5},{2,14},{3,7},{4,8},{5,1},{6,10},{7,3},{8,4},{9,13},{1... | collective-permute-start | bytes 1966088 | tf_op jit(solution)/shard_map/ppermute | solution.py:481
  85.4 9.9 %collective-permute-start.18 = (f32[32,32,128]{2,1,0:T(8,128)S(1)}, f32[32,32,128]{2,1,0:T(8,128)}, u32[]{:S(2)}, u32[]{:S(2)}) collective-permute-start(f32[32,32,128]{2,1,0:T(8,128)S(1)} %pad_maximum_fusion.2.refs_4_), channel_id=1, source_target_pairs={{0,18},{1,3},{2,16},{3,1},{4,22},{5,7},{6,20},{7,5},{8,26},{9,11},... | collective-permute-start | bytes 1572872 | tf_op jit(solution)/shard_map/ppermute | solution.py:481
  86.5 18.5 %collective-permute-start.21 = (f32[32,32,128]{2,1,0:T(8,128)S(1)}, f32[32,32,128]{2,1,0:T(8,128)S(1)}, u32[]{:S(2)}, u32[]{:S(2)}) collective-permute-start(f32[32,32,128]{2,1,0:T(8,128)S(1)} %pad_maximum_fusion.2.refs_4_), channel_id=1, source_target_pairs={{0,1},{1,0},{2,3},{3,2},{4,5},{5,4},{6,7},{7,6},{8,9},{9,8},{10,11... | collective-permute-start | bytes 1572872 | tf_op jit(solution)/shard_map/ppermute | solution.py:481
  95.3 10.6 %collective-permute-start.20 = (f32[32,40,128]{2,1,0:T(8,128)S(1)}, f32[32,40,128]{2,1,0:T(8,128)}, u32[]{:S(2)}, u32[]{:S(2)}) collective-permute-start(f32[32,40,128]{2,1,0:T(8,128)S(1)} %pad_maximum_fusion.1.refs_3_), channel_id=1, source_target_pairs={{0,1},{1,0},{2,3},{3,2},{4,5},{5,4},{6,7},{7,6},{8,9},{9,8},{10,11... | collective-permute-start | bytes 1966088 | tf_op jit(solution)/shard_map/ppermute | solution.py:481
  95.3 11.0 %collective-permute-start.19 = (f32[32,40,128]{2,1,0:T(8,128)S(1)}, f32[32,40,128]{2,1,0:T(8,128)}, u32[]{:S(2)}, u32[]{:S(2)}) collective-permute-start(f32[32,40,128]{2,1,0:T(8,128)S(1)} %pad_maximum_fusion.refs_2_), channel_id=1, source_target_pairs={{0,1},{1,0},{2,3},{3,2},{4,5},{5,4},{6,7},{7,6},{8,9},{9,8},{10,11... | collective-permute-start | bytes 1966088 | tf_op jit(solution)/shard_map/ppermute | solution.py:481
  104.5 4.5 %collective-permute-start.23 = (f32[32,40,128]{2,1,0:T(8,128)S(1)}, f32[32,40,128]{2,1,0:T(8,128)}, u32[]{:S(2)}, u32[]{:S(2)}) collective-permute-start(f32[32,40,128]{2,1,0:T(8,128)S(1)} %collective-permute-done.17.refs_6_), channel_id=1, source_target_pairs={{0,1},{1,0},{2,3},{3,2},{4,5},{5,4},{6,7},{7,6},{8,9},{9,8},{10,11... | collective-permute-start | bytes 1966088 | tf_op jit(solution)/shard_map/ppermute | solution.py:481
  104.5 4.5 %collective-permute-start.22 = (f32[32,40,128]{2,1,0:T(8,128)S(1)}, f32[32,40,128]{2,1,0:T(8,128)}, u32[]{:S(2)}, u32[]{:S(2)}) collective-permute-start(f32[32,40,128]{2,1,0:T(8,128)S(1)} %collective-permute-done.16.refs_5_), channel_id=1, source_target_pairs={{0,1},{1,0},{2,3},{3,2},{4,5},{5,4},{6,7},{7,6},{8,9},{9,8},{10,11... | collective-permute-start | bytes 1966088 | tf_op jit(solution)/shard_map/ppermute | solution.py:481
  105.0 0.8 copy-start.2
  105.8 3.2 %collective-permute-start.24 = (f32[32,32,128]{2,1,0:T(8,128)}, f32[32,32,128]{2,1,0:T(8,128)}, u32[]{:S(2)}, u32[]{:S(2)}) collective-permute-start(f32[32,32,128]{2,1,0:T(8,128)} %collective-permute-done.18.refs_7_), channel_id=1, source_target_pairs={{0,1},{1,0},{2,3},{3,2},{4,5},{5,4},{6,7},{7,6},{8,9},{9,8},{10,11... | collective-permute-start | bytes 1572872 | tf_op jit(solution)/shard_map/ppermute | solution.py:481
  109.0 1.0 copy-start.3
